TPU v7x, 32 devices: a whole 2x2x4 slice. The times are simulated.
32 devices in a mesh: section: 2 (over x), ctx: 16 (over z, y, core).
Axes of the slice: x: 2, y: 2, z: 4, core: 2. Of those that a mesh axis runs over, the one named last changes fastest.
Arguments:
- x_in: bfloat16 [512, 1536], P('ctx'), may hold values from -6 to 6
- stale_inputs: bfloat16 [2, 512, 1536], P('section', 'ctx'), may hold values from -6 to 6
- w_query: bfloat16 [2, 12, 128, 128], P('section'), may hold values from -0.5 to 0.5
- w_key: bfloat16 [2, 12, 128, 128], P('section'), may hold values from -0.5 to 0.5
- w_value: bfloat16 [2, 12, 128, 128], P('section'), may hold values from -0.5 to 0.5
- w_out: bfloat16 [2, 12, 128, 128], P('section'), may hold values from -0.5 to 0.5
- score_scale: float32 [2, 12], P('section'), may hold values from 1 to 3
- assign: int32 [512], P('ctx'), may hold values from 0 to 3, as said below
Outputs:
- section_out: bfloat16 [2, 512, 1536], P('section', 'ctx')
Inputs may be any that keep to these rules, and one draw needn't show every extreme that they name: `assign`: each aligned block of 32 tokens holds the same number of tokens of every micro-batch.
All inputs are finite; a program needn't handle non-finite values.
Results may differ from a plain program's by a relative error of at most 0.013.
Values may be sent and summed in bfloat16 or wider, within the bound.
No kernel may reach another device: no remote copies, remote signals or barrier semaphores. Data moves between devices by JAX's collectives and lax.ppermute only.
A program may use at most 128 MiB of HBM per device.

v0:
```python
import math
import jax
import jax.numpy as jnp
from jax import lax
from jax.sharding import PartitionSpec as P

MB = 4


def from_behind(array, axis, by):
    length = lax.axis_size(axis)
    pairs = [(i, i + by) for i in range(length) if 0 <= i + by < length]
    return lax.ppermute(array, axis, pairs)


def normalize(values):
    floats = values.astype(jnp.float32)
    return floats * lax.rsqrt(jnp.mean(floats * floats, axis=-1, keepdims=True) + 1e-06)


def project(normed, weight):
    count = normed.shape[0]
    return jnp.einsum(
        "nhd,hde->nhe",
        normed.reshape(count, weight.shape[0], weight.shape[1]),
        weight,
        preferred_element_type=jnp.float32,
    )


def key_pair(normed, w_key, w_value):
    count = normed.shape[0]
    keys = normalize(project(normed, w_key)).astype(jnp.bfloat16).reshape(count, -1)
    values = project(normed, w_value).astype(jnp.bfloat16).reshape(count, -1)
    return jnp.stack([keys, values])


def body(x_in, stale_inputs, w_query, w_key, w_value, w_out, score_scale, assign):
    tile_rows = x_in.shape[0]
    feature_width = x_in.shape[1]
    heads = w_query.shape[1]
    head_size = w_query.shape[2]
    query_weight = w_query[0]
    key_weight = w_key[0]
    value_weight = w_value[0]
    mix_weight = w_out[0]
    scales = score_scale[0]
    sections = lax.axis_size("section")
    section_index = lax.axis_index("section")
    ctx_index = lax.axis_index("ctx")
    per_batch = tile_rows // MB
    stale_normed = normalize(stale_inputs[0]).astype(jnp.bfloat16)
    pairs = lax.all_gather(
        key_pair(stale_normed, key_weight, value_weight), "ctx", axis=1, tiled=True
    )
    total = pairs.shape[1]
    far_keys = pairs[0].reshape(total, heads, head_size)
    far_values = pairs[1].reshape(total, heads, head_size)
    own_pair = lax.dynamic_slice_in_dim(pairs, ctx_index * tile_rows, tile_rows, 1)
    own_keys = own_pair[0].reshape(tile_rows, heads, head_size)
    own_values = own_pair[1].reshape(tile_rows, heads, head_size)
    far_mask = (jnp.arange(total, dtype=jnp.int32) // tile_rows != ctx_index).astype(jnp.float32)
    order = jnp.argsort(assign, stable=True)

    def advance(entering, batch_index, fresh_keys, fresh_values, rows):
        normed = normalize(entering).astype(jnp.bfloat16)
        queries = (
            normalize(project(normed, query_weight))
            * (scales[None, :, None] / math.sqrt(head_size))
        ).astype(jnp.bfloat16)
        new_keys = normalize(project(normed, key_weight)).astype(jnp.bfloat16)
        new_values = project(normed, value_weight).astype(jnp.bfloat16)
        fresh_keys = fresh_keys.at[rows].set(new_keys)
        fresh_values = fresh_values.at[rows].set(new_values)
        chosen = (assign <= batch_index).astype(jnp.float32)
        e_far = (
            jnp.exp(
                jnp.einsum("qhd,khd->hqk", queries, far_keys, preferred_element_type=jnp.float32)
            )
            * far_mask[None, None, :]
        )
        e_new = (
            jnp.exp(
                jnp.einsum("qhd,khd->hqk", queries, fresh_keys, preferred_element_type=jnp.float32)
            )
            * chosen[None, None, :]
        )
        e_old = (
            jnp.exp(
                jnp.einsum("qhd,khd->hqk", queries, own_keys, preferred_element_type=jnp.float32)
            )
            * (1.0 - chosen)[None, None, :]
        )
        denom = jnp.sum(e_far, -1) + jnp.sum(e_new, -1) + jnp.sum(e_old, -1)
        numer = jnp.einsum(
            "hqk,khd->qhd",
            e_far.astype(jnp.bfloat16),
            far_values,
            preferred_element_type=jnp.float32,
        )
        numer = numer + jnp.einsum(
            "hqk,khd->qhd",
            e_new.astype(jnp.bfloat16),
            fresh_values,
            preferred_element_type=jnp.float32,
        )
        numer = numer + jnp.einsum(
            "hqk,khd->qhd",
            e_old.astype(jnp.bfloat16),
            own_values,
            preferred_element_type=jnp.float32,
        )
        attended = (
            (numer / jnp.transpose(denom)[:, :, None])
            .astype(jnp.bfloat16)
            .reshape(per_batch, feature_width)
        )
        mixed = project(attended, mix_weight).reshape(per_batch, feature_width)
        return (
            (entering.astype(jnp.float32) + mixed).astype(jnp.bfloat16),
            fresh_keys,
            fresh_values,
        )

    def advance_step(moment, carry):
        incoming, out_buffer, fresh_keys, fresh_values = carry
        batch_index = moment - section_index
        valid = jnp.logical_and(batch_index >= 0, batch_index < MB)
        clamped = jnp.clip(batch_index, 0, MB - 1)
        rows = lax.dynamic_slice_in_dim(order, clamped * per_batch, per_batch)
        entering = jnp.where(section_index == 0, x_in[rows], incoming)
        result, next_keys, next_values = lax.cond(
            valid,
            lambda inputs: advance(*inputs),
            lambda inputs: (jnp.zeros_like(inputs[0]), inputs[2], inputs[3]),
            (entering, clamped, fresh_keys, fresh_values, rows),
        )
        out_buffer = jnp.where(valid, out_buffer.at[rows].set(result), out_buffer)
        incoming = from_behind(result, "section", 1)
        return (incoming, out_buffer, next_keys, next_values)

    initial = (
        jnp.zeros((per_batch, feature_width), jnp.bfloat16),
        jnp.zeros_like(x_in),
        jnp.zeros((tile_rows, heads, head_size), jnp.bfloat16),
        jnp.zeros((tile_rows, heads, head_size), jnp.bfloat16),
    )
    final = lax.fori_loop(0, MB + sections - 1, advance_step, initial)
    return final[1][None]


def solution(mesh):
    return jax.shard_map(
        body,
        mesh=mesh,
        in_specs=(
            P("ctx", None),
            P("section", "ctx", None),
            P("section", None, None, None),
            P("section", None, None, None),
            P("section", None, None, None),
            P("section", None, None, None),
            P("section", None),
            P("ctx"),
        ),
        out_specs=P("section", "ctx", None),
        check_vma=False,
    )
```

profile of v0, /device:TPU:0, one launch (start us, length us, event | category | flops | bytes accessed | tf_op | source)
XLA Modules:
  0.0 189.2 jit_solution(18121709102004149396)
XLA Ops:
  8.5 1.3 multiply_reduce_fusion.2
  12.3 2.3 %sort.17 = (s32[32]{0:T(128)}, s32[32]{0:T(128)}) sort(s32[32]{0:T(128)} %param.19, s32[32]{0:T(128)S(1)} %iota.7), dimensions={0}, to_apply=%region_0.0 | sort | flops 160 | bytes 512 | tf_op jit(solution)/shard_map/jit(argsort)/sort | solution.py:63
  14.7 46.0 %all-gather.2.cloned.1.call-done = bf16[2,512,1536]{2,1,0:T(8,128)(2,1)} async-done(((bf16[2,32,1536]{2,1,0:T(8,128)(2,1)}), bf16[2,512,1536]{2,1,0:T(8,128)(2,1)}) %all-gather.2.cloned.1.call-update) | async-done | bytes 3145744 | tf_op jit(solution)/shard_map/all_gather | solution.py:53
  63.1 3.2 %fusion.40 = (bf16[1,512,1536]{2,1,0:T(8,128)(2,1)}, bf16[1,512,1536]{2,1,0:T(8,128)(2,1)S(1)}) fusion(bf16[2,512,1536]{2,1,0:T(8,128)(2,1)} %all-gather.2.cloned.1.call-done), kind=kLoop, calls=%fused_computation.81 | loop fusion | bytes 6291456 | tf_op jit(solution)/shard_map/slice | solution.py:58
  68.0 2.6 %copy.33 = bf16[1,512,1536]{1,2,0:T(8,128)(2,1)} copy(bf16[1,512,1536]{2,1,0:T(8,128)(2,1)} %get-tuple-element.635) | data formatting | bytes 3145728 | tf_op jit(solution)/shard_map/slice | solution.py:58
  70.6 1.9 %copy.35 = bf16[512,12,128]{2,0,1:T(8,128)(2,1)S(1)} copy(bf16[512,12,128]{0,2,1:T(8,128)(2,1)} %bitcast.83) | data formatting | bytes 3145728
  73.9 107.9 %while.21 = (s32[]{:T(128)}, bf16[8,1536]{1,0:T(8,128)(2,1)S(1)}, bf16[32,1536]{1,0:T(8,128)(2,1)S(1)}, bf16[32,12,128]{2,1,0:T(8,128)(2,1)}, bf16[32,12,128]{2,...) while((s32[]{:T(128)}, bf16[8,1536]{1,0:T(8,128)(2,1)S(1)}, ...), condition=%wide.region_15.16_spmd.clone, body=%wide.region_3.15_spmd.clone.sunk | while | flops 41582888 | bytes 7045026 | solution.py:148
  74.6 15.7 %conditional.3 = (bf16[8,1536]{1,0:T(8,128)(2,1)S(1)}, bf16[32,12,128]{2,1,0:T(8,128)(2,1)}, bf16[32,12,128]{2,1,0:T(8,128)(2,1)}) conditional(s32[]{:T(128)} %convert_element_type.143, (bf16[32,12,128]{2,1,0:T(8,128)(2,1)}, bf16[32,12,128]{2,1,0:T(8,128)(2,1)}) %tuple.66, (pred[]{:T(512)}, bf16[32,1536]{1,0:T(8,128)(2,1)S(1)}, ...), branch_computations={%region_4.4_spmd, %region_5.13_spmd} | conditional | flops 41430252 | bytes 6378669 | solution.py:132
  75.4 1.3 multiply_reduce_fusion
  76.8 1.9 scatter_fusion.1
  78.7 1.3 multiply_reduce_fusion.1
  86.0 1.9 scatter_fusion
  88.9 1.4 fusion.3
  93.9 15.7 %conditional.3 = (bf16[8,1536]{1,0:T(8,128)(2,1)S(1)}, bf16[32,12,128]{2,1,0:T(8,128)(2,1)}, bf16[32,12,128]{2,1,0:T(8,128)(2,1)}) conditional(s32[]{:T(128)} %convert_element_type.143, (bf16[32,12,128]{2,1,0:T(8,128)(2,1)}, bf16[32,12,128]{2,1,0:T(8,128)(2,1)}) %tuple.66, (pred[]{:T(512)}, bf16[32,1536]{1,0:T(8,128)(2,1)S(1)}, ...), branch_computations={%region_4.4_spmd, %region_5.13_spmd} | conditional | flops 41430252 | bytes 6378669 | solution.py:132
  94.6 1.3 multiply_reduce_fusion
  96.1 1.9 scatter_fusion.1
  105.2 1.9 %scatter_fusion = bf16[32,12,128]{2,1,0:T(8,128)(2,1)} fusion(bf16[32,12,128]{2,1,0:T(8,128)(2,1)} %get-tuple-element.430, s32[8]{0:T(128)S(1)} %compare_select_fusion, bf16[8,12,128]{2,1,0:T(8,128)(2,1)S(1)} %copy.25), kind=kCustom, calls=%fused_computation.1 | custom fusion | bytes 73760 | tf_op jit(solution)/shard_map/while/body/eval_jaxpr/cond/branch_1_fun/scatter | solution.py:74
  108.2 1.4 fusion.3
  109.6 4.2 %collective-permute-start = (bf16[8,1536]{1,0:T(8,128)(2,1)S(1)}, bf16[8,1536]{1,0:T(8,128)(2,1)S(1)}, u32[]{:S(2)}, u32[]{:S(2)}) collective-permute-start(bf16[8,1536]{1,0:T(8,128)(2,1)S(1)} %get-tuple-element.772), channel_id=1, source_target_pairs={{0,16},{1,17},{2,18},{3,19},{4,20},{5,21},{6,22},{7,23},{8,24},{9,... | collective-permute-start | bytes 73736 | tf_op jit(solution)/shard_map/while/body/eval_jaxpr/ppermute | solution.py:13
  116.0 15.7 %conditional.3 = (bf16[8,1536]{1,0:T(8,128)(2,1)S(1)}, bf16[32,12,128]{2,1,0:T(8,128)(2,1)}, bf16[32,12,128]{2,1,0:T(8,128)(2,1)}) conditional(s32[]{:T(128)} %convert_element_type.143, (bf16[32,12,128]{2,1,0:T(8,128)(2,1)}, bf16[32,12,128]{2,1,0:T(8,128)(2,1)}) %tuple.66, (pred[]{:T(512)}, bf16[32,1536]{1,0:T(8,128)(2,1)S(1)}, ...), branch_computations={%region_4.4_spmd, %region_5.13_spmd} | conditional | flops 41430252 | bytes 6378669 | solution.py:132
  116.8 1.3 multiply_reduce_fusion
  118.3 1.9 scatter_fusion.1
  127.4 1.9 scatter_fusion
  130.3 1.4 fusion.3
  131.7 4.2 %collective-permute-start = (bf16[8,1536]{1,0:T(8,128)(2,1)S(1)}, bf16[8,1536]{1,0:T(8,128)(2,1)S(1)}, u32[]{:S(2)}, u32[]{:S(2)}) collective-permute-start(bf16[8,1536]{1,0:T(8,128)(2,1)S(1)} %get-tuple-element.772), channel_id=1, source_target_pairs={{0,16},{1,17},{2,18},{3,19},{4,20},{5,21},{6,22},{7,23},{8,24},{9,... | collective-permute-start | bytes 73736 | tf_op jit(solution)/shard_map/while/body/eval_jaxpr/ppermute | solution.py:13
  138.2 15.7 %conditional.3 = (bf16[8,1536]{1,0:T(8,128)(2,1)S(1)}, bf16[32,12,128]{2,1,0:T(8,128)(2,1)}, bf16[32,12,128]{2,1,0:T(8,128)(2,1)}) conditional(s32[]{:T(128)} %convert_element_type.143, (bf16[32,12,128]{2,1,0:T(8,128)(2,1)}, bf16[32,12,128]{2,1,0:T(8,128)(2,1)}) %tuple.66, (pred[]{:T(512)}, bf16[32,1536]{1,0:T(8,128)(2,1)S(1)}, ...), branch_computations={%region_4.4_spmd, %region_5.13_spmd} | conditional | flops 41430252 | bytes 6378669 | solution.py:132
  139.0 1.3 multiply_reduce_fusion
  140.4 1.9 scatter_fusion.1
  149.6 1.9 %scatter_fusion = bf16[32,12,128]{2,1,0:T(8,128)(2,1)} fusion(bf16[32,12,128]{2,1,0:T(8,128)(2,1)} %get-tuple-element.430, s32[8]{0:T(128)S(1)} %compare_select_fusion, bf16[8,12,128]{2,1,0:T(8,128)(2,1)S(1)} %copy.25), kind=kCustom, calls=%fused_computation.1 | custom fusion | bytes 73760 | tf_op jit(solution)/shard_map/while/body/eval_jaxpr/cond/branch_1_fun/scatter | solution.py:74
  152.5 1.4 fusion.3
  153.9 4.2 %collective-permute-start = (bf16[8,1536]{1,0:T(8,128)(2,1)S(1)}, bf16[8,1536]{1,0:T(8,128)(2,1)S(1)}, u32[]{:S(2)}, u32[]{:S(2)}) collective-permute-start(bf16[8,1536]{1,0:T(8,128)(2,1)S(1)} %get-tuple-element.772), channel_id=1, source_target_pairs={{0,16},{1,17},{2,18},{3,19},{4,20},{5,21},{6,22},{7,23},{8,24},{9,... | collective-permute-start | bytes 73736 | tf_op jit(solution)/shard_map/while/body/eval_jaxpr/ppermute | solution.py:13
  160.4 19.9 %collective-permute-start = (bf16[8,1536]{1,0:T(8,128)(2,1)S(1)}, bf16[8,1536]{1,0:T(8,128)(2,1)S(1)}, u32[]{:S(2)}, u32[]{:S(2)}) collective-permute-start(bf16[8,1536]{1,0:T(8,128)(2,1)S(1)} %get-tuple-element.772), channel_id=1, source_target_pairs={{0,16},{1,17},{2,18},{3,19},{4,20},{5,21},{6,22},{7,23},{8,24},{9,... | collective-permute-start | bytes 73736 | tf_op jit(solution)/shard_map/while/body/eval_jaxpr/ppermute | solution.py:13
  (150 shorter events, 58.0 us)
Async XLA Ops:
  6.5 54.1 %all-gather.2.cloned.1.call-start = ((), (), s32[]{:S(2)}) async-start(), calls=%async_computation | async-start | bytes 3342336 | tf_op jit(solution)/shard_map/all_gather | solution.py:53
  70.6 3.3 %copy-start = (bf16[32,1536]{1,0:T(8,128)(2,1)S(1)}, bf16[32,1536]{1,0:T(8,128)(2,1)}, u32[]{:S(2)}) copy-start(bf16[32,1536]{1,0:T(8,128)(2,1)} %param.12) | copy-start | bytes 294916
  90.3 2.8 %collective-permute-start = (bf16[8,1536]{1,0:T(8,128)(2,1)S(1)}, bf16[8,1536]{1,0:T(8,128)(2,1)S(1)}, u32[]{:S(2)}, u32[]{:S(2)}) collective-permute-start(bf16[8,1536]{1,0:T(8,128)(2,1)S(1)} %get-tuple-element.772), channel_id=1, source_target_pairs={{0,16},{1,17},{2,18},{3,19},{4,20},{5,21},{6,22},{7,23},{8,24},{9,... | collective-permute-start | bytes 73736 | tf_op jit(solution)/shard_map/while/body/eval_jaxpr/ppermute | solution.py:13
  109.6 5.7 %collective-permute-start = (bf16[8,1536]{1,0:T(8,128)(2,1)S(1)}, bf16[8,1536]{1,0:T(8,128)(2,1)S(1)}, u32[]{:S(2)}, u32[]{:S(2)}) collective-permute-start(bf16[8,1536]{1,0:T(8,128)(2,1)S(1)} %get-tuple-element.772), channel_id=1, source_target_pairs={{0,16},{1,17},{2,18},{3,19},{4,20},{5,21},{6,22},{7,23},{8,24},{9,... | collective-permute-start | bytes 73736 | tf_op jit(solution)/shard_map/while/body/eval_jaxpr/ppermute | solution.py:13
  131.7 5.8 %collective-permute-start = (bf16[8,1536]{1,0:T(8,128)(2,1)S(1)}, bf16[8,1536]{1,0:T(8,128)(2,1)S(1)}, u32[]{:S(2)}, u32[]{:S(2)}) collective-permute-start(bf16[8,1536]{1,0:T(8,128)(2,1)S(1)} %get-tuple-element.772), channel_id=1, source_target_pairs={{0,16},{1,17},{2,18},{3,19},{4,20},{5,21},{6,22},{7,23},{8,24},{9,... | collective-permute-start | bytes 73736 | tf_op jit(solution)/shard_map/while/body/eval_jaxpr/ppermute | solution.py:13
  153.9 5.7 %collective-permute-start = (bf16[8,1536]{1,0:T(8,128)(2,1)S(1)}, bf16[8,1536]{1,0:T(8,128)(2,1)S(1)}, u32[]{:S(2)}, u32[]{:S(2)}) collective-permute-start(bf16[8,1536]{1,0:T(8,128)(2,1)S(1)} %get-tuple-element.772), channel_id=1, source_target_pairs={{0,16},{1,17},{2,18},{3,19},{4,20},{5,21},{6,22},{7,23},{8,24},{9,... | collective-permute-start | bytes 73736 | tf_op jit(solution)/shard_map/while/body/eval_jaxpr/ppermute | solution.py:13
  160.4 21.4 %collective-permute-start = (bf16[8,1536]{1,0:T(8,128)(2,1)S(1)}, bf16[8,1536]{1,0:T(8,128)(2,1)S(1)}, u32[]{:S(2)}, u32[]{:S(2)}) collective-permute-start(bf16[8,1536]{1,0:T(8,128)(2,1)S(1)} %get-tuple-element.772), channel_id=1, source_target_pairs={{0,16},{1,17},{2,18},{3,19},{4,20},{5,21},{6,22},{7,23},{8,24},{9,... | collective-permute-start | bytes 73736 | tf_op jit(solution)/shard_map/while/body/eval_jaxpr/ppermute | solution.py:13
  181.8 0.6 copy-start.1
Sparse Core Ops, SparseCore 0:
  12.4 48.1 all-gather.1
where the time goes:
time: 191 us; the launch traced here: 189 us
  waiting for transfers between devices  49.4 us (26%)
  matrix products  40.7 us (21%)
  local copies, waits for them, and re-layouts  36.2 us (19%)
  starting transfers between devices  33.8 us (18%)
  other arithmetic  15 us (8%)
  between operations  13.5 us (7%)
    all_gather x1, waiting for transfers between devices, body(): lax.all_gather(key_pair(stale_normed, key_weight, value_weight), 'ctx', a...  46 us
    ppermute x5, starting transfers between devices, from_behind(): return lax.ppermute(array, axis, pairs)  33.8 us
    dot_general x18, matrix products, project(): jnp.einsum('nhd,hde->nhe', normed.reshape(count, weight.shape[0], weight....  23.7 us
    scatter x4, local copies, waits for them, and re-layouts, advance(): fresh_values = fresh_values.at[rows].set(new_values)  7.57 us
    scatter x4, local copies, waits for them, and re-layouts, advance(): fresh_keys = fresh_keys.at[rows].set(new_keys)  7.53 us
    slice x2, local copies, waits for them, and re-layouts, body(): far_values = pairs[1].reshape(total, heads, head_size)  5.84 us
    unnamed x8, local copies, waits for them, and re-layouts  4.81 us
    dot_general x4, matrix products, advance(): jnp.einsum('qhd,khd->hqk', queries, fresh_keys, preferred_element_type=jn...  4.58 us
  transfers between devices with their start and end apart: 6, of which 6 were waited for; matrix products, arithmetic and copies ran while one was open for 3% of the time, Pallas kernels for 0%

commit v1 on v0

--- a/solution.py
+++ b/solution.py
@@ -50,9 +50,10 @@
     ctx_index = lax.axis_index("ctx")
     per_batch = tile_rows // MB
     stale_normed = normalize(stale_inputs[0]).astype(jnp.bfloat16)
-    pairs = lax.all_gather(
-        key_pair(stale_normed, key_weight, value_weight), "ctx", axis=1, tiled=True
-    )
+    shard = key_pair(stale_normed, key_weight, value_weight)
+    size = lax.axis_size("ctx")
+    repeats = [size if d == 1 else 1 for d in range(shard.ndim)]
+    pairs = lax.all_to_all(jnp.tile(shard, repeats), "ctx", split_axis=1, concat_axis=1, tiled=True)
     total = pairs.shape[1]
     far_keys = pairs[0].reshape(total, heads, head_size)
     far_values = pairs[1].reshape(total, heads, head_size)

time: 191 us -> 223 us (1.17)
  the two profiles are of different devices: /device:TPU:0 before, /device:TPU:18 now
where the time goes in v1:
time: 223 us; the launch traced here: 221 us
  waiting for transfers between devices  99.3 us (45%)
  local copies, waits for them, and re-layouts  56.5 us (25%)
  matrix products  40.8 us (18%)
  starting transfers between devices  12.8 us (6%)
  other arithmetic  11.1 us (5%)
    all_to_all x1, waiting for transfers between devices, body(): lax.all_to_all(jnp.tile(shard, repeats), 'ctx', split_axis=1, concat_axis...  68.4 us
    ppermute x5, waiting for transfers between devices, from_behind(): return lax.ppermute(array, axis, pairs)  30.9 us
    dot_general x18, matrix products, project(): jnp.einsum('nhd,hde->nhe', normed.reshape(count, weight.shape[0], weight....  23.7 us
    unnamed x13, local copies, waits for them, and re-layouts  19.1 us
    scatter x4, local copies, waits for them, and re-layouts, advance(): fresh_values = fresh_values.at[rows].set(new_values)  7.56 us
    scatter x4, local copies, waits for them, and re-layouts, advance(): fresh_keys = fresh_keys.at[rows].set(new_keys)  7.55 us
    ppermute x5, starting transfers between devices, from_behind(): return lax.ppermute(array, axis, pairs)  6.46 us
    all_to_all x1, starting transfers between devices, body(): lax.all_to_all(jnp.tile(shard, repeats), 'ctx', split_axis=1, concat_axis...  6.32 us
  transfers between devices with their start and end apart: 6, of which 6 were waited for; matrix products, arithmetic and copies ran while one was open for 3% of the time, Pallas kernels for 0%

profile of v1, /device:TPU:18, one launch (start us, length us, event | category | flops | bytes accessed | tf_op | source)
XLA Modules:
  0.0 221.1 jit_solution(8948234922913682497)
XLA Ops:
  2.0 1.3 multiply_reduce_fusion.2
  5.4 4.9 %copy.62 = bf16[2,512,1536]{2,0,1:T(2,128)(2,1)} copy(bf16[2,512,1536]{2,1,0:T(8,128)(2,1)S(1)} %bitcast.91) | data formatting | bytes 6291456 | tf_op jit(solution)/shard_map/tile | solution.py:56
  10.3 6.3 %all-to-all-start = ((bf16[2,512,1536]{2,0,1:T(2,128)(2,1)}), bf16[2,512,1536]{2,0,1:T(2,128)(2,1)S(1)}, u32[]{:S(2)}, u32[]{:S(2)}) async-start(bf16[2,512,1536]{2,0,1:T(2,128)(2,1)} %copy.62), calls=%async_computation | async-start | bytes 6291456 | tf_op jit(solution)/shard_map/all_to_all | solution.py:56
  16.7 1.7 sort.17
  18.4 68.4 %all-to-all-done = bf16[2,512,1536]{2,0,1:T(2,128)(2,1)S(1)} async-done(((bf16[2,512,1536]{2,0,1:T(2,128)(2,1)}), bf16[2,512,1536]{2,0,1:T(2,128)(2,1)S(1)}, u32[]{:S(2)}, u32[]{:S(2)}) %all-to-all-start) | async-done | bytes 3145760 | tf_op jit(solution)/shard_map/all_to_all | solution.py:56
  86.7 6.3 %fusion.40 = (bf16[1,512,1536]{2,0,1:T(2,128)(2,1)}, bf16[1,512,1536]{2,0,1:T(2,128)(2,1)}) fusion(bf16[2,512,1536]{2,0,1:T(2,128)(2,1)S(1)} %all-to-all-done), kind=kLoop, calls=%fused_computation.83 | loop fusion | bytes 6291456 | tf_op jit(solution)/shard_map/slice | solution.py:59
  93.0 6.8 %copy.69 = bf16[1,512,1536]{1,2,0:T(8,128)(2,1)S(1)} copy(bf16[1,512,1536]{2,0,1:T(2,128)(2,1)} %get-tuple-element.676) | data formatting | bytes 3145728
  100.7 8.1 %copy.70 = bf16[1,512,1536]{1,2,0:T(8,128)(2,1)} copy(bf16[1,512,1536]{2,0,1:T(2,128)(2,1)} %get-tuple-element.675) | data formatting | bytes 3145728
  108.9 1.9 copy.66
  110.8 2.1 dynamic-slice_reduce_fusion
  115.0 105.5 %while.21 = (s32[]{:T(128)}, bf16[8,1536]{1,0:T(8,128)(2,1)S(1)}, bf16[32,1536]{1,0:T(8,128)(2,1)S(1)}, bf16[32,12,128]{2,1,0:T(8,128)(2,1)}, bf16[32,12,128]{2,...) while((s32[]{:T(128)}, bf16[8,1536]{1,0:T(8,128)(2,1)S(1)}, ...), condition=%wide.region_15.16_spmd.clone, body=%wide.region_3.15_spmd.clone.sunk | while | flops 41582888 | bytes 7045026 | solution.py:149
  117.9 16.5 %collective-permute-done = bf16[8,1536]{1,0:T(8,128)(2,1)S(1)} collective-permute-done((bf16[8,1536]{1,0:T(8,128)(2,1)S(1)}, bf16[8,1536]{1,0:T(8,128)(2,1)S(1)}, u32[]{:S(2)}, u32[]{:S(2)}) %collective-permute-start) | collective-permute-done | bytes 24608 | tf_op jit(solution)/shard_map/while/body/eval_jaxpr/ppermute | solution.py:13
  135.1 15.0 %conditional.3 = (bf16[8,1536]{1,0:T(8,128)(2,1)S(1)}, bf16[32,12,128]{2,1,0:T(8,128)(2,1)}, bf16[32,12,128]{2,1,0:T(8,128)(2,1)}) conditional(s32[]{:T(128)} %convert_element_type.143, (bf16[32,12,128]{2,1,0:T(8,128)(2,1)}, bf16[32,12,128]{2,1,0:T(8,128)(2,1)}) %tuple.69, (pred[]{:T(512)}, bf16[32,1536]{1,0:T(8,128)(2,1)S(1)}, ...), branch_computations={%region_4.4_spmd, %region_5.13_spmd} | conditional | flops 41430252 | bytes 6378669 | solution.py:133
  137.3 1.9 scatter_fusion.1
  145.9 1.9 scatter_fusion
  148.8 1.4 fusion.3
  152.3 3.6 %collective-permute-done = bf16[8,1536]{1,0:T(8,128)(2,1)S(1)} collective-permute-done((bf16[8,1536]{1,0:T(8,128)(2,1)S(1)}, bf16[8,1536]{1,0:T(8,128)(2,1)S(1)}, u32[]{:S(2)}, u32[]{:S(2)}) %collective-permute-start) | collective-permute-done | bytes 24608 | tf_op jit(solution)/shard_map/while/body/eval_jaxpr/ppermute | solution.py:13
  156.7 15.0 %conditional.3 = (bf16[8,1536]{1,0:T(8,128)(2,1)S(1)}, bf16[32,12,128]{2,1,0:T(8,128)(2,1)}, bf16[32,12,128]{2,1,0:T(8,128)(2,1)}) conditional(s32[]{:T(128)} %convert_element_type.143, (bf16[32,12,128]{2,1,0:T(8,128)(2,1)}, bf16[32,12,128]{2,1,0:T(8,128)(2,1)}) %tuple.69, (pred[]{:T(512)}, bf16[32,1536]{1,0:T(8,128)(2,1)S(1)}, ...), branch_computations={%region_4.4_spmd, %region_5.13_spmd} | conditional | flops 41430252 | bytes 6378669 | solution.py:133
  158.9 1.9 scatter_fusion.1
  167.4 1.9 scatter_fusion
  170.3 1.4 fusion.3
  173.8 3.6 %collective-permute-done = bf16[8,1536]{1,0:T(8,128)(2,1)S(1)} collective-permute-done((bf16[8,1536]{1,0:T(8,128)(2,1)S(1)}, bf16[8,1536]{1,0:T(8,128)(2,1)S(1)}, u32[]{:S(2)}, u32[]{:S(2)}) %collective-permute-start) | collective-permute-done | bytes 24608 | tf_op jit(solution)/shard_map/while/body/eval_jaxpr/ppermute | solution.py:13
  178.2 15.1 %conditional.3 = (bf16[8,1536]{1,0:T(8,128)(2,1)S(1)}, bf16[32,12,128]{2,1,0:T(8,128)(2,1)}, bf16[32,12,128]{2,1,0:T(8,128)(2,1)}) conditional(s32[]{:T(128)} %convert_element_type.143, (bf16[32,12,128]{2,1,0:T(8,128)(2,1)}, bf16[32,12,128]{2,1,0:T(8,128)(2,1)}) %tuple.69, (pred[]{:T(512)}, bf16[32,1536]{1,0:T(8,128)(2,1)S(1)}, ...), branch_computations={%region_4.4_spmd, %region_5.13_spmd} | conditional | flops 41430252 | bytes 6378669 | solution.py:133
  180.4 1.9 scatter_fusion.1
  188.9 1.9 scatter_fusion
  191.9 1.4 fusion.3
  195.4 3.6 %collective-permute-done = bf16[8,1536]{1,0:T(8,128)(2,1)S(1)} collective-permute-done((bf16[8,1536]{1,0:T(8,128)(2,1)S(1)}, bf16[8,1536]{1,0:T(8,128)(2,1)S(1)}, u32[]{:S(2)}, u32[]{:S(2)}) %collective-permute-start) | collective-permute-done | bytes 24608 | tf_op jit(solution)/shard_map/while/body/eval_jaxpr/ppermute | solution.py:13
  199.7 15.0 %conditional.3 = (bf16[8,1536]{1,0:T(8,128)(2,1)S(1)}, bf16[32,12,128]{2,1,0:T(8,128)(2,1)}, bf16[32,12,128]{2,1,0:T(8,128)(2,1)}) conditional(s32[]{:T(128)} %convert_element_type.143, (bf16[32,12,128]{2,1,0:T(8,128)(2,1)}, bf16[32,12,128]{2,1,0:T(8,128)(2,1)}) %tuple.69, (pred[]{:T(512)}, bf16[32,1536]{1,0:T(8,128)(2,1)S(1)}, ...), branch_computations={%region_4.4_spmd, %region_5.13_spmd} | conditional | flops 41430252 | bytes 6378669 | solution.py:133
  201.9 1.9 scatter_fusion.1
  210.4 1.9 scatter_fusion
  213.4 1.4 fusion.3
  216.9 3.6 %collective-permute-done = bf16[8,1536]{1,0:T(8,128)(2,1)S(1)} collective-permute-done((bf16[8,1536]{1,0:T(8,128)(2,1)S(1)}, bf16[8,1536]{1,0:T(8,128)(2,1)S(1)}, u32[]{:S(2)}, u32[]{:S(2)}) %collective-permute-start) | collective-permute-done | bytes 24608 | tf_op jit(solution)/shard_map/while/body/eval_jaxpr/ppermute | solution.py:13
  (152 shorter events, 61.0 us)
Async XLA Ops:
  10.3 6.3 %copy-start.3 = (s32[32]{0:T(128)S(1)}, s32[32]{0:T(128)}, u32[]{:S(2)}) copy-start(s32[32]{0:T(128)} %param.19) | copy-start | bytes 388
  10.3 76.4 %all-to-all-start = ((bf16[2,512,1536]{2,0,1:T(2,128)(2,1)}), bf16[2,512,1536]{2,0,1:T(2,128)(2,1)S(1)}, u32[]{:S(2)}, u32[]{:S(2)}) async-start(bf16[2,512,1536]{2,0,1:T(2,128)(2,1)} %copy.62), calls=%async_computation | async-start | bytes 6291456 | tf_op jit(solution)/shard_map/all_to_all | solution.py:56
  86.7 6.3 %copy-start = (bf16[2,512,1536]{2,0,1:T(2,128)(2,1)}, bf16[2,512,1536]{2,0,1:T(2,128)(2,1)S(1)}, u32[]{:S(2)}) copy-start(bf16[2,512,1536]{2,0,1:T(2,128)(2,1)S(1)} %all-to-all-done) | copy-start | bytes 9437188
  108.9 6.1 %copy-start.1 = (bf16[32,1536]{1,0:T(8,128)(2,1)S(1)}, bf16[32,1536]{1,0:T(8,128)(2,1)}, u32[]{:S(2)}) copy-start(bf16[32,1536]{1,0:T(8,128)(2,1)} %param.12) | copy-start | bytes 294916
  115.8 18.6 %collective-permute-start = (bf16[8,1536]{1,0:T(8,128)(2,1)S(1)}, bf16[8,1536]{1,0:T(8,128)(2,1)S(1)}, u32[]{:S(2)}, u32[]{:S(2)}) collective-permute-start(bf16[8,1536]{1,0:T(8,128)(2,1)S(1)} %get-tuple-element.814), channel_id=1, source_target_pairs={{0,16},{1,17},{2,18},{3,19},{4,20},{5,21},{6,22},{7,23},{8,24},{9,... | collective-permute-start | bytes 73736 | tf_op jit(solution)/shard_map/while/body/eval_jaxpr/ppermute | solution.py:13
  150.2 5.7 %collective-permute-start = (bf16[8,1536]{1,0:T(8,128)(2,1)S(1)}, bf16[8,1536]{1,0:T(8,128)(2,1)S(1)}, u32[]{:S(2)}, u32[]{:S(2)}) collective-permute-start(bf16[8,1536]{1,0:T(8,128)(2,1)S(1)} %get-tuple-element.814), channel_id=1, source_target_pairs={{0,16},{1,17},{2,18},{3,19},{4,20},{5,21},{6,22},{7,23},{8,24},{9,... | collective-permute-start | bytes 73736 | tf_op jit(solution)/shard_map/while/body/eval_jaxpr/ppermute | solution.py:13
  171.7 5.7 %collective-permute-start = (bf16[8,1536]{1,0:T(8,128)(2,1)S(1)}, bf16[8,1536]{1,0:T(8,128)(2,1)S(1)}, u32[]{:S(2)}, u32[]{:S(2)}) collective-permute-start(bf16[8,1536]{1,0:T(8,128)(2,1)S(1)} %get-tuple-element.814), channel_id=1, source_target_pairs={{0,16},{1,17},{2,18},{3,19},{4,20},{5,21},{6,22},{7,23},{8,24},{9,... | collective-permute-start | bytes 73736 | tf_op jit(solution)/shard_map/while/body/eval_jaxpr/ppermute | solution.py:13
  193.2 5.7 %collective-permute-start = (bf16[8,1536]{1,0:T(8,128)(2,1)S(1)}, bf16[8,1536]{1,0:T(8,128)(2,1)S(1)}, u32[]{:S(2)}, u32[]{:S(2)}) collective-permute-start(bf16[8,1536]{1,0:T(8,128)(2,1)S(1)} %get-tuple-element.814), channel_id=1, source_target_pairs={{0,16},{1,17},{2,18},{3,19},{4,20},{5,21},{6,22},{7,23},{8,24},{9,... | collective-permute-start | bytes 73736 | tf_op jit(solution)/shard_map/while/body/eval_jaxpr/ppermute | solution.py:13
  214.8 5.7 %collective-permute-start = (bf16[8,1536]{1,0:T(8,128)(2,1)S(1)}, bf16[8,1536]{1,0:T(8,128)(2,1)S(1)}, u32[]{:S(2)}, u32[]{:S(2)}) collective-permute-start(bf16[8,1536]{1,0:T(8,128)(2,1)S(1)} %get-tuple-element.814), channel_id=1, source_target_pairs={{0,16},{1,17},{2,18},{3,19},{4,20},{5,21},{6,22},{7,23},{8,24},{9,... | collective-permute-start | bytes 73736 | tf_op jit(solution)/shard_map/while/body/eval_jaxpr/ppermute | solution.py:13
  220.5 0.6 copy-start.2
